TPU v7x, 256 devices: a whole 4x4x8 slice. The times are simulated.
256 devices in a mesh: inner: 8 (over x, core), outer: 32 (over z, y).
Axes of the slice: x: 4, y: 4, z: 8, core: 2. Of those that a mesh axis runs over, the one named last changes fastest.
Arguments:
- queries: bfloat16 [32768, 2048], P(('outer', 'inner')), may hold values from -6 to 6
- keys: bfloat16 [32768, 2048], P(('outer', 'inner')), may hold values from -6 to 6
- values: bfloat16 [32768, 2048], P(('outer', 'inner')), may hold values from -6 to 6
- out_grad: bfloat16 [32768, 2048], P(('outer', 'inner')), may hold values from -6 to 6
- positions: int32 [32768], P(('outer', 'inner')), may hold values from 0 to 8191
Outputs:
- attended: bfloat16 [32768, 2048], P(('outer', 'inner'))
- query_grad: bfloat16 [32768, 2048], P(('outer', 'inner'))
- key_grad: bfloat16 [32768, 2048], P(('outer', 'inner'))
- value_gradient: bfloat16 [32768, 2048], P(('outer', 'inner'))
All inputs are finite; a program needn't handle non-finite values.
Results may differ from a plain program's by a relative error of at most 0.0064.
Values sent between devices are 32-bit elements; how exact they have to be, the bound alone decides.
A program may use at most 256 MiB of HBM per device.

v0:
```python
import math
import jax
import jax.numpy as jnp
from jax import lax
from jax.sharding import PartitionSpec as P

D_HEAD = 128


def carried_in(value, axis, join, neutral, backward):
    count, mine = (lax.axis_size(axis), lax.axis_index(axis))
    pieces = lax.all_gather(value, axis)
    if backward:
        pieces = pieces[::-1]
        mine = count - 1 - mine
    so_far = jnp.full_like(value, 0) + jnp.asarray(neutral, value.dtype)

    def step(position, so_far):
        longer = join(so_far, pieces[position])
        return jnp.where(position < mine, longer, so_far)

    return lax.fori_loop(0, count - 1, step, so_far)


def rotary_tables(positions, head_dim):
    half_dim = head_dim // 2
    spacing = jnp.arange(half_dim).astype(jnp.float32) * (-2.0 * math.log(500000.0) / head_dim)
    angle = positions.astype(jnp.float32)[:, None] * jnp.exp(spacing)[None, :]
    return (jnp.cos(angle)[:, None, :], jnp.sin(angle)[:, None, :])


def rotate(rows, cosine, sine):
    half_dim = rows.shape[-1] // 2
    first = rows[..., :half_dim].astype(jnp.float32)
    second = rows[..., half_dim:].astype(jnp.float32)
    return jnp.concatenate(
        [first * cosine - second * sine, second * cosine + first * sine], axis=-1
    )


def unrotate(rows, cosine, sine):
    half_dim = rows.shape[-1] // 2
    first = rows[..., :half_dim]
    second = rows[..., half_dim:]
    return jnp.concatenate(
        [first * cosine + second * sine, second * cosine - first * sine], axis=-1
    )


def add_states(earlier, later):
    return earlier + later


def outer_sums(keys_group, queries_group):
    zero_part = jnp.zeros_like(keys_group)
    keys_earlier = carried_in(keys_group, "outer", add_states, zero_part, False)
    queries_later = carried_in(queries_group, "outer", add_states, zero_part, True)
    return (keys_earlier, queries_later)


def shards(queries, keys, values, out_grad, positions):
    rows_here = queries.shape[0]
    head_dim = D_HEAD
    heads_count = queries.shape[1] // head_dim
    total_tokens = rows_here * lax.axis_size("inner") * lax.axis_size("outer")
    scale_factor = (head_dim * total_tokens) ** (-0.5)
    cosine, sine = rotary_tables(positions, head_dim)
    shaped = (rows_here, heads_count, head_dim)
    rotated_query = rotate(queries.reshape(shaped), cosine, sine).astype(jnp.bfloat16)
    rotated_key = rotate(keys.reshape(shaped), cosine, sine).astype(jnp.bfloat16)
    value_row_block = values.reshape(shaped)
    gradient_row_block = out_grad.reshape(shaped)
    key_value_state = jnp.einsum(
        "pob,poj->obj", rotated_key, value_row_block, preferred_element_type=jnp.float32
    )
    query_state = jnp.einsum(
        "pob,poj->obj", rotated_query, gradient_row_block, preferred_element_type=jnp.float32
    )
    own_place = lax.axis_index("inner")
    piece = (
        lax.all_gather(key_value_state[None], "inner", axis=0, tiled=True),
        lax.all_gather(query_state[None], "inner", axis=0, tiled=True),
    )
    count = piece[0].shape[0]
    order = jnp.arange(count, dtype=jnp.int32)
    earlier = (order < own_place)[:, None, None, None]
    later = (order > own_place)[:, None, None, None]
    keys_before = jnp.sum(jnp.where(earlier, piece[0], 0.0), axis=0)
    queries_after = jnp.sum(jnp.where(later, piece[1], 0.0), axis=0)
    keys_group = jnp.sum(piece[0], axis=0)
    queries_group = jnp.sum(piece[1], axis=0)
    keys_earlier, queries_later = outer_sums(keys_group, queries_group)
    preceding_state = (keys_earlier + keys_before).astype(jnp.bfloat16)
    following_state = (queries_later + queries_after).astype(jnp.bfloat16)
    causal = (jnp.arange(rows_here)[:, None] >= jnp.arange(rows_here)[None, :])[None]
    score_matrix = jnp.where(
        causal,
        jnp.einsum("thd,shd->hts", rotated_query, rotated_key, preferred_element_type=jnp.float32),
        0.0,
    ).astype(jnp.bfloat16)
    score_gradient = jnp.where(
        causal,
        jnp.einsum(
            "thd,shd->hts", gradient_row_block, value_row_block, preferred_element_type=jnp.float32
        ),
        0.0,
    ).astype(jnp.bfloat16)
    attended = scale_factor * (
        jnp.einsum(
            "rgb,brf->grf", score_matrix, value_row_block, preferred_element_type=jnp.float32
        )
        + jnp.einsum(
            "axz,xzo->axo", rotated_query, preceding_state, preferred_element_type=jnp.float32
        )
    )
    rotated_query_gradient = scale_factor * (
        jnp.einsum("rgb,brf->grf", score_gradient, rotated_key, preferred_element_type=jnp.float32)
        + jnp.einsum(
            "xge,gme->xgm", gradient_row_block, preceding_state, preferred_element_type=jnp.float32
        )
    )
    rotated_key_gradient = scale_factor * (
        jnp.einsum(
            "uox,oul->xul", score_gradient, rotated_query, preferred_element_type=jnp.float32
        )
        + jnp.einsum(
            "olb,lfb->olf", value_row_block, following_state, preferred_element_type=jnp.float32
        )
    )
    value_gradient = scale_factor * (
        jnp.einsum(
            "uox,oul->xul", score_matrix, gradient_row_block, preferred_element_type=jnp.float32
        )
        + jnp.einsum(
            "tyg,yge->tye", rotated_key, following_state, preferred_element_type=jnp.float32
        )
    )
    flat = (rows_here, heads_count * head_dim)
    return (
        attended.astype(jnp.bfloat16).reshape(flat),
        unrotate(rotated_query_gradient, cosine, sine).astype(jnp.bfloat16).reshape(flat),
        unrotate(rotated_key_gradient, cosine, sine).astype(jnp.bfloat16).reshape(flat),
        value_gradient.astype(jnp.bfloat16).reshape(flat),
    )


def solution(mesh):
    placed = (
        P(("outer", "inner"), None),
        P(("outer", "inner"), None),
        P(("outer", "inner"), None),
        P(("outer", "inner"), None),
        P(("outer", "inner")),
    )
    return jax.shard_map(
        shards,
        mesh=mesh,
        in_specs=placed,
        out_specs=(
            P(("outer", "inner"), None),
            P(("outer", "inner"), None),
            P(("outer", "inner"), None),
            P(("outer", "inner"), None),
        ),
        check_vma=False,
    )
```

profile of v0, /device:TPU:1, one launch (start us, length us, event | category | flops | bytes accessed | tf_op | source)
XLA Modules:
  0.0 743.1 jit_solution(15101625095384080709)
XLA Ops:
  13.8 56.5 %all-gather.13.cloned.1.call-done = f32[128,128,128]{2,1,0:T(8,128)} async-done(((f32[16,128,128]{2,1,0:T(8,128)}), f32[128,128,128]{2,1,0:T(8,128)}) %all-gather.13.cloned.1.call-update) | async-done | bytes 8388624 | tf_op jit(solution)/shard_map/all_gather | solution.py:82
  70.3 6.1 select_reduce_fusion
  78.6 2.0 copy.101
  83.4 225.2 %all-gather.15.cloned.1.call-done = f32[512,128,128]{2,1,0:T(8,128)} async-done(((f32[16,128,128]{2,1,0:T(8,128)}), f32[512,128,128]{2,1,0:T(8,128)}) %all-gather.15.cloned.1.call-update) | async-done | bytes 33554448 | tf_op jit(solution)/shard_map/all_gather | solution.py:12
  308.6 23.0 %rev.3 = f32[32,16,128,128]{3,2,1,0:T(8,128)} reverse(f32[32,16,128,128]{3,2,1,0:T(8,128)} %bitcast.85), dimensions={0} | reverse | bytes 67108864 | tf_op jit(solution)/shard_map/rev | solution.py:14
  331.6 50.0 %while.29 = (s32[]{:T(128)}, f32[16,128,128]{2,1,0:T(8,128)S(1)}, s32[]{:T(128)}, f32[32,16,128,128]{3,2,1,0:T(8,128)}, s32[]{:T(128)}, /*index=5*/s32[]{:T(128)}) while((s32[]{:T(128)}, f32[16,128,128]{2,1,0:T(8,128)S(1)}, s32[]{:T(128)}, f32[32,16,128,128]{3,2,1,0:T(8,128)}, s32[]{:T(128)}, /*index=5*/s32[]{:T(128)}) %tuple.77), condition=%wide.region_6.7_spmd.clone, body=%wide.region_5.6_spmd.clone.sunk | while | flops 786436 | bytes 3145821 | solution.py:22
  333.2 1.6 add_select_fusion.5
  334.8 1.6 add_select_fusion.5
  339.7 1.6 add_select_fusion.5
  341.3 1.6 add_select_fusion.5
  342.9 1.6 add_select_fusion.5
  346.1 1.6 add_select_fusion.5
  347.7 1.6 add_select_fusion.5
  349.4 1.6 add_select_fusion.5
  351.0 1.6 add_select_fusion.5
  354.2 1.6 add_select_fusion.5
  355.8 1.6 add_select_fusion.5
  357.4 1.6 add_select_fusion.5
  362.3 1.6 add_select_fusion.5
  383.0 1.9 fusion.5
  384.9 2.6 add_convert_fusion
  389.5 50.3 %all-gather.9.cloned.1.call-done = f32[128,128,128]{2,1,0:T(8,128)} async-done(((f32[16,128,128]{2,1,0:T(8,128)}), f32[128,128,128]{2,1,0:T(8,128)}) %all-gather.9.cloned.1.call-update) | async-done | bytes 8388624 | tf_op jit(solution)/shard_map/all_gather | solution.py:81
  439.8 6.1 select_reduce_fusion.1
  446.4 1.7 convolution_bitcast_fusion.1
  449.3 2.0 copy.88
  451.3 2.3 pad_maximum_fusion.3
  453.6 2.0 copy.82
  455.7 2.0 copy.87
  457.7 2.6 convolution_bitcast_fusion.3
  460.3 217.8 %all-gather.11.cloned.1.call-done = f32[512,128,128]{2,1,0:T(8,128)} async-done(((f32[16,128,128]{2,1,0:T(8,128)}), f32[512,128,128]{2,1,0:T(8,128)}) %all-gather.11.cloned.1.call-update) | async-done | bytes 33554448 | tf_op jit(solution)/shard_map/all_gather | solution.py:12
  678.1 50.0 %while.28 = (s32[]{:T(128)}, f32[16,128,128]{2,1,0:T(8,128)S(1)}, s32[]{:T(128)}, f32[32,16,128,128]{3,2,1,0:T(8,128)}, s32[]{:T(128)}, /*index=5*/s32[]{:T(128)}) while((s32[]{:T(128)}, f32[16,128,128]{2,1,0:T(8,128)S(1)}, s32[]{:T(128)}, f32[32,16,128,128]{3,2,1,0:T(8,128)}, s32[]{:T(128)}, /*index=5*/s32[]{:T(128)}) %tuple.91), condition=%wide.region_2.3_spmd.clone, body=%wide.region_1.2_spmd.clone.sunk | while | flops 786436 | bytes 3145821 | solution.py:22
  733.7 1.9 fusion.8
  (101 shorter events, 100.9 us)
Async XLA Ops:
  7.2 74.4 %copy-start = (bf16[128,2048]{1,0:T(8,128)(2,1)S(1)}, bf16[128,2048]{1,0:T(8,128)(2,1)}, u32[]{:S(2)}) copy-start(bf16[128,2048]{1,0:T(8,128)(2,1)} %param.11) | copy-start | bytes 1572868
  7.2 63.1 %all-gather.13.cloned.1.call-start = ((), (), s32[]{:S(2)}) async-start(), calls=%async_computation.2 | async-start | bytes 9437184 | tf_op jit(solution)/shard_map/all_gather | solution.py:82
  13.8 294.8 %all-gather.15.cloned.1.call-start = ((), (), s32[]{:S(2)}) async-start(), calls=%async_computation.3 | async-start | bytes 34603008 | tf_op jit(solution)/shard_map/all_gather | solution.py:12
  76.4 363.4 %all-gather.9.cloned.1.call-start = ((), (), s32[]{:S(2)}) async-start(), calls=%async_computation | async-start | bytes 9437184 | tf_op jit(solution)/shard_map/all_gather | solution.py:81
  82.1 249.5 %copy-start.4 = (bf16[16,128,128]{2,1,0:T(8,128)(2,1)}, bf16[16,128,128]{2,1,0:T(8,128)(2,1)S(1)}, u32[]{:S(2)}) copy-start(bf16[16,128,128]{2,1,0:T(8,128)(2,1)S(1)} %fusion.11) | copy-start | bytes 1572868
  383.0 62.9 %copy-start.3 = (bf16[16,128,128]{2,1,0:T(8,128)(2,1)}, bf16[16,128,128]{2,1,0:T(8,128)(2,1)S(1)}, u32[]{:S(2)}) copy-start(bf16[16,128,128]{2,1,0:T(8,128)(2,1)S(1)} %add_convert_fusion.1) | copy-start | bytes 1572868
  389.2 288.8 %all-gather.11.cloned.1.call-start = ((), (), s32[]{:S(2)}) async-start(), calls=%async_computation.1 | async-start | bytes 34603008 | tf_op jit(solution)/shard_map/all_gather | solution.py:12
  446.4 1.8 copy-start.2
  729.5 0.8 copy-start.1
Sparse Core Ops, SparseCore 0:
  13.9 56.3 all-gather.12
  76.6 232.0 all-gather.14
  389.4 50.3 all-gather.8
  446.0 232.0 all-gather.10
where the time goes:
time: 746 us; the launch traced here: 743 us
  waiting for transfers between devices  550 us (74%)
  other arithmetic  121 us (16%)
  local copies, waits for them, and re-layouts  40 us (5%)
  matrix products  16.5 us (2%)
  between operations  14 us (2%)
    all_gather x2, waiting for transfers between devices, carried_in(): pieces = lax.all_gather(value, axis)  443 us
    select_n x62, other arithmetic, step(): return jnp.where(position < mine, longer, so_far)  98.5 us
    all_gather x1, waiting for transfers between devices, shards(): lax.all_gather(query_state[None], 'inner', axis=0, tiled=True)  56.5 us
    all_gather x1, waiting for transfers between devices, shards(): lax.all_gather(key_value_state[None], 'inner', axis=0, tiled=True)  50.3 us
    rev x1, local copies, waits for them, and re-layouts, carried_in(): pieces = pieces[::-1]  23 us
  transfers between devices with their start and end apart: 4, of which 4 were waited for; matrix products, arithmetic and copies ran while one was open for 3% of the time, Pallas kernels for 0%

commit v1 on v0

--- a/solution.py
+++ b/solution.py
@@ -79,7 +79,10 @@
     own_place = lax.axis_index("inner")
     piece = (
         lax.all_gather(key_value_state[None], "inner", axis=0, tiled=True),
-        lax.all_gather(query_state[None], "inner", axis=0, tiled=True),
+        jnp.concatenate(
+            lax.all_to_all(jnp.stack([query_state[None]] * lax.axis_size("inner")), "inner", 0, 0),
+            axis=0,
+        ),
     )
     count = piece[0].shape[0]
     order = jnp.arange(count, dtype=jnp.int32)

time: 746 us -> 790 us (1.059)
  blocking collectives: 0 us -> 100 us
  waiting for transfers between devices: 550 us -> 489 us
    all_to_all x0 -> x1, blocking collectives: none -> 100 us  [shards(): lax.all_to_all(jnp.stack([query_state[None]] * lax.axis_size('inner')), '...]
    all_gather x1 -> x0, waiting for transfers between devices: 56.5 us -> none  [shards(): lax.all_gather(query_state[None], 'inner', axis=0, tiled=True)]
  transfers between devices with their start and end apart: 4 -> 3, of which waited for: 4 -> 3; matrix products, arithmetic and copies ran while one was open for 3% -> 3% of each run, Pallas kernels for 0% -> 0%
where the time goes in v1:
time: 790 us; the launch traced here: 787 us
  waiting for transfers between devices  489 us (62%)
  other arithmetic  126 us (16%)
  blocking collectives  100 us (13%)
  local copies, waits for them, and re-layouts  40.7 us (5%)
  matrix products  15.2 us (2%)
  between operations  14 us (2%)
    all_gather x2, waiting for transfers between devices, carried_in(): pieces = lax.all_gather(value, axis)  439 us
    all_to_all x1, blocking collectives, shards(): lax.all_to_all(jnp.stack([query_state[None]] * lax.axis_size('inner')), '...  100 us
    select_n x62, other arithmetic, step(): return jnp.where(position < mine, longer, so_far)  98.5 us
    all_gather x1, waiting for transfers between devices, shards(): lax.all_gather(key_value_state[None], 'inner', axis=0, tiled=True)  50.3 us
    rev x1, local copies, waits for them, and re-layouts, carried_in(): pieces = pieces[::-1]  23 us
  transfers between devices with their start and end apart: 3, of which 3 were waited for; matrix products, arithmetic and copies ran while one was open for 3% of the time, Pallas kernels for 0%

profile of v1, /device:TPU:1, one launch (start us, length us, event | category | flops | bytes accessed | tf_op | source)
XLA Modules:
  0.0 786.6 jit_solution(8633407626280688745)
XLA Ops:
  13.7 100.2 %all_to_all.5 = f32[8,1,16,128,128]{4,3,2,1,0:T(8,128)} all-to-all(f32[8,1,16,128,128]{4,3,2,1,0:T(8,128)S(1)} %stack.3), channel_id=1, replica_groups=mesh['inner'=8,'outer'=32] {'inner'}, dimensions={0} | all-to-all | bytes 16777216 | tf_op jit(solution)/shard_map/all_to_all | solution.py:83
  114.0 5.2 reduce_sum.38
  121.3 2.0 copy.102
  126.1 5.5 fusion
  131.7 220.9 %all-gather.11.cloned.1.call-done = f32[512,128,128]{2,1,0:T(8,128)} async-done(((f32[16,128,128]{2,1,0:T(8,128)}), f32[512,128,128]{2,1,0:T(8,128)}) %all-gather.11.cloned.1.call-update) | async-done | bytes 33554448 | tf_op jit(solution)/shard_map/all_gather | solution.py:12
  352.6 23.0 %rev.3 = f32[32,16,128,128]{3,2,1,0:T(8,128)} reverse(f32[32,16,128,128]{3,2,1,0:T(8,128)} %bitcast.88), dimensions={0} | reverse | bytes 67108864 | tf_op jit(solution)/shard_map/rev | solution.py:14
  375.6 50.0 %while.29 = (s32[]{:T(128)}, f32[16,128,128]{2,1,0:T(8,128)S(1)}, s32[]{:T(128)}, f32[32,16,128,128]{3,2,1,0:T(8,128)}, s32[]{:T(128)}, /*index=5*/s32[]{:T(128)}) while((s32[]{:T(128)}, f32[16,128,128]{2,1,0:T(8,128)S(1)}, s32[]{:T(128)}, f32[32,16,128,128]{3,2,1,0:T(8,128)}, s32[]{:T(128)}, /*index=5*/s32[]{:T(128)}) %tuple.76), condition=%wide.region_6.7_spmd.clone, body=%wide.region_5.6_spmd.clone.sunk | while | flops 786436 | bytes 3145829 | solution.py:22
  378.8 1.6 add_select_fusion.5
  380.4 1.6 add_select_fusion.5
  382.0 1.6 add_select_fusion.5
  386.9 1.6 add_select_fusion.5
  388.5 1.6 add_select_fusion.5
  390.1 1.6 add_select_fusion.5
  393.3 1.6 add_select_fusion.5
  394.9 1.6 add_select_fusion.5
  396.5 1.6 add_select_fusion.5
  398.2 1.6 add_select_fusion.5
  401.4 1.6 add_select_fusion.5
  403.0 1.6 add_select_fusion.5
  426.9 1.9 fusion.6
  428.8 2.6 add_convert_fusion
  433.5 50.3 %all-gather.7.cloned.1.call-done = f32[128,128,128]{2,1,0:T(8,128)} async-done(((f32[16,128,128]{2,1,0:T(8,128)}), f32[128,128,128]{2,1,0:T(8,128)}) %all-gather.7.cloned.1.call-update) | async-done | bytes 8388624 | tf_op jit(solution)/shard_map/all_gather | solution.py:81
  483.8 6.1 select_reduce_fusion
  489.9 2.3 pad_maximum_fusion.3
  492.2 2.0 copy.82
  494.2 2.0 copy.87
  496.8 1.7 convolution_bitcast_fusion.1
  499.6 2.0 copy.88
  501.7 2.6 convolution_bitcast_fusion.3
  504.3 217.7 %all-gather.9.cloned.1.call-done = f32[512,128,128]{2,1,0:T(8,128)} async-done(((f32[16,128,128]{2,1,0:T(8,128)}), f32[512,128,128]{2,1,0:T(8,128)}) %all-gather.9.cloned.1.call-update) | async-done | bytes 33554448 | tf_op jit(solution)/shard_map/all_gather | solution.py:12
  722.1 50.0 %while.28 = (s32[]{:T(128)}, f32[16,128,128]{2,1,0:T(8,128)S(1)}, s32[]{:T(128)}, f32[32,16,128,128]{3,2,1,0:T(8,128)}, s32[]{:T(128)}, /*index=5*/s32[]{:T(128)}) while((s32[]{:T(128)}, f32[16,128,128]{2,1,0:T(8,128)S(1)}, s32[]{:T(128)}, f32[32,16,128,128]{3,2,1,0:T(8,128)}, s32[]{:T(128)}, /*index=5*/s32[]{:T(128)}) %tuple.88), condition=%wide.region_2.3_spmd.clone, body=%wide.region_1.2_spmd.clone.sunk | while | flops 786436 | bytes 3145829 | solution.py:22
  774.0 1.7 fusion.9
  (99 shorter events, 102.1 us)
Async XLA Ops:
  7.2 117.1 %copy-start = (bf16[128,2048]{1,0:T(8,128)(2,1)S(1)}, bf16[128,2048]{1,0:T(8,128)(2,1)}, u32[]{:S(2)}) copy-start(bf16[128,2048]{1,0:T(8,128)(2,1)} %param.11) | copy-start | bytes 1572868
  7.2 345.4 %all-gather.11.cloned.1.call-start = ((), (), s32[]{:S(2)}) async-start(), calls=%async_computation.3 | async-start | bytes 34603008 | tf_op jit(solution)/shard_map/all_gather | solution.py:12
  119.2 364.6 %all-gather.7.cloned.1.call-start = ((), (), s32[]{:S(2)}) async-start(), calls=%async_computation.1 | async-start | bytes 9437184 | tf_op jit(solution)/shard_map/all_gather | solution.py:81
  124.8 250.8 %copy-start.3 = (bf16[16,128,128]{2,1,0:T(8,128)(2,1)}, bf16[16,128,128]{2,1,0:T(8,128)(2,1)S(1)}, u32[]{:S(2)}) copy-start(bf16[16,128,128]{2,1,0:T(8,128)(2,1)S(1)} %fusion.12) | copy-start | bytes 1572868
  426.9 62.9 %copy-start.2 = (bf16[16,128,128]{2,1,0:T(8,128)(2,1)}, bf16[16,128,128]{2,1,0:T(8,128)(2,1)S(1)}, u32[]{:S(2)}) copy-start(bf16[16,128,128]{2,1,0:T(8,128)(2,1)S(1)} %add_convert_fusion.1) | copy-start | bytes 1572868
  433.2 288.9 %all-gather.9.cloned.1.call-start = ((), (), s32[]{:S(2)}) async-start(), calls=%async_computation.2 | async-start | bytes 34603008 | tf_op jit(solution)/shard_map/all_gather | solution.py:12
  496.7 1.8 copy-start.1
Sparse Core Ops, SparseCore 0:
  119.3 233.2 all-gather.10
  433.3 50.3 all-gather.6
  490.0 232.0 all-gather.8
